TPU v7x, 256 devices: a whole 4x4x8 slice. The times are simulated.
256 devices in a mesh: grp: 16 (over y, x), tp: 16 (over z, core).
Axes of the slice: x: 4, y: 4, z: 8, core: 2. Of those that a mesh axis runs over, the one named last changes fastest.
Arguments:
- hidden: bfloat16 [294912, 5120], P(('grp', 'tp')), may hold values from -6 to 6
- lengths: int32 [16, 16], P('grp'), may hold values from 1 to 1152, 7372 in all within a row
- kv_weight: bfloat16 [5120, 1024], P('grp', 'tp'), may hold values from -0.078125 to 0.078125
- input_gain: float32 [5120], replicated, may hold values from 0.1 to 1.9
- key_gain: float32 [128], replicated, may hold values from 0.1 to 1.9
Outputs:
- cache_pages: bfloat16 [1280, 128, 1024], P(('grp', 'tp'))
Inputs may be any that keep to these rules, and one draw needn't show every extreme that they name: In each group's row the 16 lengths sum to 7372 and the largest equals 1152.
All inputs are finite; a program needn't handle non-finite values.
Results may differ from a plain program's by a relative error of at most 0.0049.
Values may be sent and summed in bfloat16 or wider, within the bound.
A program may use at most 64 MiB of HBM per device.

v0:
```python
import math

import jax
import jax.numpy as jnp
from jax import lax
from jax.sharding import PartitionSpec as P

HD = 128
KVH = 4
BLK = 128


rope_base = 1000000.0
norm_eps = 1e-06


def normalize(token_rows, input_gain):
    values = token_rows.astype(jnp.float32)
    row_scale = lax.rsqrt(jnp.mean(values * values, axis=-1, keepdims=True) + norm_eps)
    return (values * row_scale * input_gain).astype(jnp.bfloat16)


def finish(projected, positions, valid, key_gain):
    key_width = KVH * HD
    half_dim = HD // 2
    row_count = projected.shape[0]
    key_part = projected[:, :key_width].reshape(row_count, KVH, HD)
    key_scale = lax.rsqrt(jnp.mean(key_part * key_part, axis=-1, keepdims=True) + norm_eps)
    key_part = key_part * key_scale * key_gain
    exponent = jnp.arange(half_dim, dtype=jnp.float32) * (2.0 / HD)
    inverse = jnp.exp(exponent * -math.log(rope_base))
    angles = positions.astype(jnp.float32)[:, None] * inverse[None, :]
    cosine = jnp.cos(angles)[:, None, :]
    sine_part = jnp.sin(angles)[:, None, :]
    lower_half = key_part[..., :half_dim]
    upper_half = key_part[..., half_dim:]
    turned = jnp.concatenate(
        [
            lower_half * cosine - upper_half * sine_part,
            upper_half * cosine + lower_half * sine_part,
        ],
        axis=-1,
    )
    merged = jnp.concatenate(
        [turned.reshape(row_count, key_width), projected[:, key_width:]], axis=-1
    )
    return jnp.where(valid[:, None], merged, 0.0).astype(jnp.bfloat16)


def project(normed, kv_weight):
    all_rows = lax.all_gather(kv_weight, "grp", axis=0, tiled=True)
    return jnp.dot(
        normed,
        lax.all_gather(all_rows, "tp", axis=1, tiled=True),
        preferred_element_type=jnp.float32,
    )


def local(hidden, lengths, kv_weight, input_gain, key_gain):
    tp_count = lax.axis_size("tp")
    my_index = lax.axis_index("tp")
    own_blocks = hidden.shape[0] // BLK
    live_tokens = 2 * tp_count * own_blocks * BLK // 5
    page_count = ((live_tokens + BLK - 1) // BLK + 2 * tp_count - 2) // tp_count
    per_peer = (own_blocks + tp_count - 1) // tp_count
    cache_width = 2 * KVH * HD
    group_len = lengths[0]
    block_counts = (group_len + (BLK - 1)) // BLK
    block_ends = jnp.cumsum(block_counts)
    block_starts = block_ends - block_counts
    offsets = jnp.arange(BLK, dtype=jnp.int32)
    my_start = block_starts[my_index]
    my_count = block_counts[my_index]
    my_length = group_len[my_index]
    outbound = (
        jnp.arange(tp_count, dtype=jnp.int32)[:, None] - my_start
    ) % tp_count + tp_count * jnp.arange(per_peer, dtype=jnp.int32)[None, :]
    outbound = outbound.reshape(-1)
    sending = outbound < my_count
    picked_local = jnp.minimum(outbound, own_blocks - 1)
    page_ranks = tp_count * jnp.arange(page_count, dtype=jnp.int32) + my_index
    anchor = jnp.minimum(
        jnp.sum((block_ends[None, :] <= page_ranks[:, None]).astype(jnp.int32), axis=1),
        tp_count - 1,
    )
    block_index = page_ranks - block_starts[anchor]
    page_live = page_ranks < block_ends[-1]
    chosen = anchor * per_peer + jnp.clip(block_index // tp_count, 0, per_peer - 1)
    projected = project(normalize(hidden, input_gain), kv_weight)
    own_pos = (jnp.arange(own_blocks, dtype=jnp.int32)[:, None] * BLK + offsets[None, :]).reshape(
        -1
    )
    own_cache = finish(projected, own_pos, own_pos < my_length, key_gain).reshape(
        own_blocks, BLK, cache_width
    )
    outgoing = jnp.where(
        sending[:, None, None],
        jnp.take(own_cache, picked_local, axis=0),
        jnp.zeros((), jnp.bfloat16),
    )
    arrived = lax.all_to_all(outgoing, "tp", split_axis=0, concat_axis=0, tiled=True)
    cache_pages = jnp.take(arrived, chosen, axis=0)
    return jnp.where(page_live[:, None, None], cache_pages, jnp.zeros((), jnp.bfloat16))


def solution(mesh):
    placed = (P(("grp", "tp"), None), P("grp", None), P("grp", "tp"), P(), P())
    return jax.shard_map(
        local, mesh=mesh, in_specs=placed, out_specs=P(("grp", "tp"), None, None), check_vma=False
    )
```

profile of v0, /device:TPU:1, one launch (start us, length us, event | category | flops | bytes accessed | tf_op | source)
XLA Modules:
  0.0 249.6 jit_solution(15077039572765754980)
XLA Ops:
  6.5 20.4 %all-gather = bf16[16,320,64]{1,2,0:T(8,128)(2,1)S(1)} all-gather(bf16[1,320,64]{1,2,0:T(8,128)(2,1)} %bitcast.44), channel_id=1, replica_groups=mesh['grp'=16,'tp'=16] {'grp'}, dimensions={0}, use_global_device_ids=true | all-gather | bytes 696320 | tf_op jit(solution)/shard_map/all_gather | solution.py:51
  27.4 1.5 reshape.400
  31.6 1.8 compare_and_fusion
  34.0 0.6 fusion.8
  34.7 6.7 %fusion = f32[1152]{0:T(1024)S(1)} fusion(bf16[1152,5120]{1,0:T(8,128)(2,1)} %param.5), kind=kLoop, calls=%fused_computation.5 | loop fusion | flops 17693568 | bytes 11801088 | tf_op jit(solution)/shard_map/reduce_sum | solution.py:19
  41.4 3.5 %multiply_cosine_fusion = (f32[1152,64]{1,0:T(8,128)}, f32[1152,64]{1,0:T(8,128)}) fusion(f32[64]{0:T(128)S(1)} %multiply_exponential_fusion, f32[1152]{0:T(1024)S(1)} %convert_bitcast_fusion), kind=kLoop, calls=%fused_computation.21 | loop fusion | flops 73728 | bytes 594688 | tf_op jit(solution)/shard_map/cos | solution.py:33
  44.9 56.4 %all-gather.3.cloned.1.call-done = bf16[5120,1024]{0,1:T(8,128)(2,1)} async-done(((bf16[5120,64]{0,1:T(8,128)(2,1)}), bf16[5120,1024]{0,1:T(8,128)(2,1)}) %all-gather.3.cloned.1.call-update) | async-done | bytes 10485776 | tf_op jit(solution)/shard_map/all_gather | solution.py:54
  101.3 16.9 %fusion.3 = f32[1152,1024]{1,0:T(8,128)S(1)} fusion(bf16[5120,1024]{0,1:T(8,128)(2,1)} %all-gather.3.cloned.1.call-done, bf16[1152,5120]{1,0:T(8,128)(2,1)} %param.5, f32[5120]{0:T(1024)S(1)} %copy-done.8, f32[1152]{0:T(1024)S(1)} %add_rsqrt_fusion.1), kind=kOutput, calls=%fused_computation.8 | convolution fusion | flops 12103188480 | bytes 27025920 | tf_op jit(solution)/shard_map/dot_general | solution.py:52
  118.2 1.7 slice.28
  120.1 2.6 %reshape.374 = f32[1152,4,128]{2,1,0:T(4,128)S(1)} reshape(f32[1152,512]{1,0:T(8,128)} %slice.28) | data formatting | bytes 4718592 | tf_op jit(solution)/shard_map/reshape | solution.py:27
  122.7 2.0 multiply_reduce_fusion
  124.9 1.5 multiply_multiply_fusion
  126.4 1.8 multiply_subtract_fusion
  128.3 1.7 pad_maximum_fusion
  129.9 1.3 concatenate.12
  131.2 1.7 fusion.7
  132.9 2.9 %gather_fusion.1 = bf16[16,128,1024]{2,1,0:T(8,128)(2,1)} fusion(bf16[9,128,1024]{2,1,0:T(8,128)(2,1)S(1)} %fusion.7, s32[1024]{0:T(1024)} %pad_clamp_fusion.1), kind=kCustom, calls=%fused_computation.1 | custom fusion | bytes 8388672 | tf_op jit(solution)/shard_map/jit(_take)/gather | solution.py:98
  135.8 4.7 %select_select_fusion = bf16[16,128,1024]{2,1,0:T(8,128)(2,1)} fusion(bf16[16,128,1024]{2,1,0:T(8,128)(2,1)} %gather_fusion.1, pred[16]{0:T(512)(128)(4,1)S(1)} %copy-done.2, pred[16]{0:T(512)(128)(4,1)S(1)} %copy-done.3), kind=kLoop, calls=%fused_computation.13 | loop fusion | flops 4194304 | bytes 8388640 | tf_op jit(solution)/shard_map/jit(_where)/select_n | solution.py:96
  140.5 4.7 %all-to-all-start = ((bf16[16,128,1024]{2,1,0:T(8,128)(2,1)}), bf16[16,128,1024]{2,1,0:T(8,128)(2,1)}, u32[]{:S(2)}, u32[]{:S(2)}) async-start(bf16[16,128,1024]{2,1,0:T(8,128)(2,1)} %select_select_fusion), calls=%async_computation | async-start | bytes 8388608 | tf_op jit(solution)/shard_map/all_to_all | solution.py:101
  145.9 0.6 gather_fusion
  146.5 0.7 compare_and_fusion.1
  147.2 91.5 %all-to-all-done = bf16[16,128,1024]{2,1,0:T(8,128)(2,1)} async-done(((bf16[16,128,1024]{2,1,0:T(8,128)(2,1)}), bf16[16,128,1024]{2,1,0:T(8,128)(2,1)}, u32[]{:S(2)}, u32[]{:S(2)}) %all-to-all-start) | async-done | bytes 4194336 | tf_op jit(solution)/shard_map/all_to_all | solution.py:101
  238.7 2.8 %gather_fusion.2 = bf16[5,128,1024]{2,1,0:T(8,128)(2,1)S(1)} fusion(bf16[16,128,1024]{2,1,0:T(8,128)(2,1)} %all-to-all-done, s32[1024]{0:T(1024)S(1)} %pad_clamp_fusion), kind=kCustom, calls=%fused_computation.2 | custom fusion | bytes 2621460 | tf_op jit(solution)/shard_map/jit(_take)/gather | solution.py:102
  241.5 1.3 select_select_fusion.1
  (44 shorter events, 4.8 us)
Async XLA Ops:
  6.5 22.4 %copy-start.7 = (s32[1,16]{1,0:T(1,128)S(1)}, s32[1,16]{1,0:T(1,128)}, u32[]{:S(2)}) copy-start(s32[1,16]{1,0:T(1,128)} %param.6) | copy-start | bytes 196
  6.5 94.7 %all-gather.3.cloned.1.call-start = ((), (), s32[]{:S(2)}) async-start(), calls=%async_computation.1 | async-start | bytes 11141120 | tf_op jit(solution)/shard_map/all_gather | solution.py:54
  29.8 4.9 %copy-start.4 = (s32[16]{0:T(128)}, s32[16]{0:T(128)S(1)}, u32[]{:S(2)}) copy-start(s32[16]{0:T(128)S(1)} %reduce) | copy-start | bytes 196
  34.7 66.6 %copy-start.8 = (f32[5120]{0:T(1024)S(1)}, f32[5120]{0:T(1024)}, u32[]{:S(2)}) copy-start(f32[5120]{0:T(1024)} %param.8) | copy-start | bytes 61444
  122.7 2.1 copy-start.6
  124.9 1.5 copy-start
  124.9 1.5 copy-start.1
  132.9 2.9 %copy-start.2 = (pred[16]{0:T(512)(128)(4,1)S(1)}, pred[16]{0:T(512)(128)(4,1)}, u32[]{:S(2)}) copy-start(pred[16]{0:T(512)(128)(4,1)} %get-tuple-element.13) | copy-start | bytes 52
  132.9 2.9 %copy-start.3 = (pred[16]{0:T(512)(128)(4,1)S(1)}, pred[16]{0:T(512)(128)(4,1)}, u32[]{:S(2)}) copy-start(pred[16]{0:T(512)(128)(4,1)} %get-tuple-element.14) | copy-start | bytes 52
  140.5 5.2 %copy-start.5 = (s32[16]{0:T(128)S(1)}, s32[16]{0:T(128)}, u32[]{:S(2)}) copy-start(s32[16]{0:T(128)} %copy-done.4) | copy-start | bytes 196
  140.5 98.2 %all-to-all-start = ((bf16[16,128,1024]{2,1,0:T(8,128)(2,1)}), bf16[16,128,1024]{2,1,0:T(8,128)(2,1)}, u32[]{:S(2)}, u32[]{:S(2)}) async-start(bf16[16,128,1024]{2,1,0:T(8,128)(2,1)} %select_select_fusion), calls=%async_computation | async-start | bytes 8388608 | tf_op jit(solution)/shard_map/all_to_all | solution.py:101
Sparse Core Ops, SparseCore 0:
  29.1 72.1 all-gather.2
where the time goes:
time: 250 us
  waiting for transfers between devices  148 us (59%)
  other arithmetic  29.7 us (12%)
  blocking collectives  20.4 us (8%)
  matrix products  16.9 us (7%)
  local copies, waits for them, and re-layouts  16.5 us (7%)
  between operations  13.6 us (5%)
  starting transfers between devices  4.66 us (2%)
    all_to_all x1, waiting for transfers between devices, local(): lax.all_to_all(outgoing, 'tp', split_axis=0, concat_axis=0, tiled=True)  91.5 us
    all_gather x1, waiting for transfers between devices, project(): lax.all_gather(all_rows, 'tp', axis=1, tiled=True)  56.4 us
    all_gather x1, blocking collectives, project(): all_rows = lax.all_gather(kv_weight, 'grp', axis=0, tiled=True)  20.4 us
    dot_general x1, matrix products, project(): jnp.dot(normed, lax.all_gather(all_rows, 'tp', axis=1, tiled=True), prefe...  16.9 us
    reduce_sum x1, other arithmetic, normalize(): jnp.mean(values * values, axis=-1, keepdims=True) + norm_eps  6.71 us
  transfers between devices with their start and end apart: 2, of which 2 were waited for; matrix products, arithmetic and copies ran while one was open for 7% of the time, Pallas kernels for 0%

commit v1 on v0

v1 whole, which is shorter than its diff:
```python
import functools
import math

import jax
import jax.numpy as jnp
import numpy as np
from jax import lax
from jax.experimental import pallas as pl
from jax.experimental.pallas import tpu as pltpu
from jax.sharding import PartitionSpec as P

HD = 128
BLK = 128
NB = 9
NZ = 8
PAGES = 5
NC = 8
EPS = 1e-06
MESH = pl.DeviceIdType.MESH
BF, F32, I32 = jnp.bfloat16, jnp.float32, jnp.int32

CA = (5, 4, 3, 2)
CB = (4, 3, 2)
SRC = 10
BASE_A = tuple(SRC + sum(CA[:i]) for i in range(4))
BASE_B = tuple(SRC + sum(CA) + sum(CB[:i]) for i in range(3))
ZERO = SRC + sum(CA) + sum(CB)
T_LEN, T_P, T_O, T_A, T_B, T_F = 0, 1, 6, 11, 16, 20
T_SIZE = 32


def tables(first, length, z, c, where):
    d = 1 - 2 * c
    seq = 2 * z + c

    def begin(zz):
        return (first(2 * zz) - c + 1) >> 1

    out = {T_LEN: length}
    fs = first(seq)
    for e in range(5):
        b = ((fs + 1 - c) & 1) + 2 * e
        out[T_P + e] = where(b > NB - 1, NB - 1, b)
        b = ((fs + c) & 1) + 2 * e
        out[T_O + e] = where(b > NB - 1, NB - 1, b)
    m0, m1 = begin(z), begin(z + 1)
    q0 = ((first(2 * z + 1) - c + 1) >> 1) - m0

    def source_index(u):
        lead = u < q0
        v = where(c == 0, where(lead, u, 5 + u - q0), where(lead, 5 + u, u - q0))
        v = where(v < 0, 0, v)
        return where(v > SRC - 1, SRC - 1, v)

    for base, slots, order in ((T_A, CA[0], (4, 3, 2, 1)), (T_B, CB[0], (5, 6, 7))):
        pos = 0
        table = [0] * slots
        for kap in order:
            first_m = m0 + ((z + d * kap - m0) & 7)
            for e in range(2):
                m = first_m + 8 * e
                present = m < m1
                value = source_index(m - m0)
                for q in range(slots):
                    table[q] = where(present & (pos == q), value, table[q])
                pos = pos + where(present, 1, 0)
        for q in range(slots):
            out[base + q] = table[q]
    total = first(2 * NZ)
    begins = [begin(i) for i in range(NZ + 1)]
    for s in range(PAGES):
        m = 8 * s + z
        zs = 0
        for i in range(NZ - 1):
            zs = zs + where(begins[i + 1] <= m, 1, 0)
        s0, s1 = begins[0], begins[1]
        for i in range(1, NZ):
            s0 = where(zs == i, begins[i], s0)
            s1 = where(zs == i, begins[i + 1], s1)
        kap = (d * (z - zs)) & 7
        second = where(m - 8 >= s0, 1, 0)

        def count(k):
            f = s0 + ((zs + d * k - s0) & 7)
            return where(f < s1, 1, 0) + where(f + 8 < s1, 1, 0)

        value = source_index(m - m0)
        pos = second
        for k in (4, 3, 2, 1):
            value = where(kap == k, BASE_A[k - 1] + pos, value)
            pos = pos + count(k)
        pos = second
        for k in (5, 6, 7):
            value = where(kap == k, BASE_B[7 - k] + pos, value)
            pos = pos + count(k)
        out[T_F + s] = where(16 * s + 2 * z + c < total, value, ZERO)
    return out


def table_kernel(len_ref, tab_ref, first_ref):
    t = lax.axis_index("tp")
    z, c = t // 2, t % 2
    running = jnp.int32(0)
    first_ref[0] = running
    for i in range(2 * NZ):
        running = running + ((len_ref[0, i] + (BLK - 1)) >> 7)
        first_ref[i + 1] = running
    out = tables(lambda i: first_ref[i], len_ref[0, t], z, c, jnp.where)
    for i in range(T_SIZE):
        tab_ref[i] = jnp.asarray(out.get(i, 0), I32)


def main_kernel(ny, nx, rows, depth, *refs):
    (tab, wp, kg, cs_hbm, x_hbm, out,
     xv, csv, rs, W, pairb, own, acc, src, fin, stp, prv, sta, stb,
     ra1, ra2, ra3, ra4, rb1, rb2, rb3,
     x_sem, cs_sem, pair_s, pair_r, z_s, z_r, p1_s, p1_r, p2_s, p2_r, h_s, h_r, a2a_s, a2a_r) = refs
    ra, rb = (ra1, ra2, ra3, ra4), (rb1, rb2, rb3)
    half = depth // (ny * nx * 2)
    g, t = lax.axis_index("grp"), lax.axis_index("tp")
    z, c = t // 2, t % 2
    y, x = g // nx, g % nx
    d = 1 - 2 * c

    def dev(gg, tt):
        return {"grp": gg, "tp": tt}

    partner = dev(g, t + d)
    z_peers = [dev(g, 2 * ((z + k) % NZ) + c) for k in range(1, NZ)]
    far = dev(g, 2 * ((z + d + NZ) % NZ) + c)
    near = dev(g, 2 * ((z - d + NZ) % NZ) + c)
    x_peers = [dev(y * nx + (x + k) % nx, t) for k in range(1, nx)]
    y_peers = [dev(((y + k) % ny) * nx + x, t) for k in range(1, ny)]

    def x_copy(b):
        rows_b = pl.ds(pl.multiple_of(b * BLK, BLK), BLK)
        return pltpu.make_async_copy(x_hbm.at[rows_b], xv.at[rows_b], x_sem.at[b])

    cs_copy = pltpu.make_async_copy(cs_hbm, csv, cs_sem)

    @pl.loop(0, NB)
    def _(b):
        x_copy(b).start()

    cs_copy.start()

    barrier = pltpu.get_barrier_semaphore()
    everyone = [partner, *z_peers, *x_peers, *y_peers]
    for p in everyone:
        pl.semaphore_signal(barrier, inc=1, device_id=p, device_id_type=MESH)
    pl.semaphore_wait(barrier, len(everyone))

    def remote(s, r, ss, rr, p):
        return pltpu.make_async_remote_copy(
            src_ref=s, dst_ref=r, send_sem=ss, recv_sem=rr, device_id=p, device_id_type=MESH
        )

    pair_copy = remote(
        wp.at[pl.ds(pl.multiple_of((1 - c) * half, half), half)], pairb, pair_s, pair_r, partner
    )
    pair_copy.start()
    pair_copy.wait_recv()
    mine = wp[pl.ds(pl.multiple_of(c * half, half), half)]
    W[z, y, x, c] = mine + pairb[...]

    def z_copy(k):
        return remote(W.at[z, y, x, c], W.at[z, y, x, c], z_s.at[k], z_r.at[z], z_peers[k])

    for k in (0, NZ - 2, 1, NZ - 3, 2, NZ - 4, 3):
        z_copy(k).start()

    def piece(n, yy, xx):
        return W.at[n, yy, xx, c]

    def at_x(k):
        return (y, (x + k) % nx)

    def at_y(k):
        return ((y + k) % ny, x)

    def pick(a, b):
        return jax.tree.map(lambda i, j: jnp.where(c == 0, i, j), a, b)

    np1, np2 = nx - 1, ny - 1
    first_peer = [pick(x_peers[k], y_peers[k]) for k in range(np1)]
    second_peer = [pick(y_peers[k], x_peers[k]) for k in range(np2)]

    def p1_copy(n, k):
        return remote(piece(n, y, x), piece(n, y, x), p1_s.at[n, k], p1_r.at[n, k], first_peer[k])

    def p2_copy(n, j, l):
        yy, xx = (y, x) if j == 0 else pick(at_x(nx - j), at_y(ny - j))
        return remote(piece(n, yy, xx), piece(n, yy, xx), p2_s.at[n, j, l], p2_r.at[n], second_peer[l])

    def phase1(n):
        @pl.when(n != z)
        def _():
            pltpu.make_async_copy(W.at[0, 0, 0, 0], W.at[0, 0, 0, 0], z_r.at[n]).wait()

        for k in range(np1):
            p1_copy(n, k).start()
        for l in range(np2):
            p2_copy(n, 0, l).start()

    def phase2(n):
        for k in range(np1):
            pltpu.make_async_copy(W.at[0, 0, 0, 0], W.at[0, 0, 0, 0], p1_r.at[n, k]).wait()
            for l in range(np2):
                p2_copy(n, k + 1, l).start()

    def hand_copy(n):
        return remote(W.at[n, :, :, c], W.at[n, :, :, c], h_s.at[n], h_r.at[n], partner)

    def hand_over(n):
        if np2:
            dummy = W.at[0, pl.ds(0, np2), :, 0]
            pltpu.make_async_copy(dummy, dummy, p2_r.at[n]).wait()
        hand_copy(n).start()

    phase1(0)
    phase1(1)
    phase1(2)
    phase2(0)
    phase2(1)

    length = tab[T_LEN]

    @pl.loop(0, NB)
    def _(b):
        x_copy(b).wait()

        @pl.loop(0, BLK // 16)
        def _(i):
            r0 = pl.multiple_of(b * BLK + i * 16, 16)
            v = xv[pl.ds(r0, 16), :].astype(F32)
            mean = jnp.sum(v * v, axis=1, keepdims=True) * (1.0 / depth)
            scale = jnp.broadcast_to(lax.rsqrt(mean + EPS), (16, HD))
            p = r0 + lax.broadcasted_iota(I32, (16, HD), 0)
            rs[pl.ds(r0, 16), :] = jnp.where(p < length, scale, 0.0)

    cs_copy.wait()
    hand_over(0)
    fin[ZERO] = jnp.zeros((BLK, HD), BF)

    def compute(n):
        tile = 3 * BLK

        @pl.loop(0, NB // 3)
        def _(i):
            r0 = pl.multiple_of(i * tile, tile)
            rows_i = pl.ds(r0, tile)
            w = W[n].reshape(depth, HD)
            a = jnp.dot(xv[rows_i, :], w, preferred_element_type=F32)
            acc[...] = a * rs[rows_i, :]

            @pl.when(n < NC // 2)
            def _():
                k = acc[...]
                s = lax.rsqrt(jnp.mean(k * k, axis=1, keepdims=True) + EPS)
                k = k * s * kg[...]
                turned = k * csv[0, rows_i, :] + pltpu.roll(k, HD // 2, 1) * csv[1, rows_i, :]
                own[pl.ds(3 * i, 3)] = turned.astype(BF).reshape(3, BLK, HD)

            @pl.when(n >= NC // 2)
            def _():
                own[pl.ds(3 * i, 3)] = acc[...].astype(BF).reshape(3, BLK, HD)

    def pair_block_copy(n):
        return remote(stp.at[n], prv.at[n], a2a_s.at[n, 0], a2a_r.at[n, 0], partner)

    def hop_a(n, h):
        s = sta.at[n] if h == 0 else ra[h - 1].at[n, pl.ds(0, CA[h])]
        return remote(s, ra[h].at[n], a2a_s.at[n, 1 + h], a2a_r.at[n, 1 + h], far)

    def hop_b(n, h):
        s = stb.at[n] if h == 0 else rb[h - 1].at[n, pl.ds(0, CB[h])]
        return remote(s, rb[h].at[n], a2a_s.at[n, 5 + h], a2a_r.at[n, 5 + h], near)

    def send_first(n):
        for e in range(5):
            stp[n, e] = own[tab[T_P + e]]
        pair_block_copy(n).start()
        for e in range(5):
            src[n, e] = own[tab[T_O + e]]
        pair_block_copy(n).wait_recv()
        for e in range(5):
            src[n, 5 + e] = prv[n, e]
            fin[e] = src[n, e]
            fin[5 + e] = prv[n, e]
        for q in range(CA[0]):
            sta[n, q] = fin[tab[T_A + q]]
        for q in range(CB[0]):
            stb[n, q] = fin[tab[T_B + q]]
        hop_a(n, 0).start()
        hop_b(n, 0).start()

    def forward(n, h):
        hop_a(n, h - 1).wait_recv()
        if h < 4:
            hop_a(n, h).start()
        if h - 1 < 3:
            hop_b(n, h - 1).wait_recv()
        if h < 3:
            hop_b(n, h).start()

    def assemble(n):
        for e in range(SRC):
            fin[e] = src[n, e]
        for h in range(4):
            for q in range(CA[h]):
                fin[BASE_A[h] + q] = ra[h][n, q]
        for h in range(3):
            for q in range(CB[h]):
                fin[BASE_B[h] + q] = rb[h][n, q]
        columns = pl.ds(pl.multiple_of(n * HD, HD), HD)
        for s in range(PAGES):
            out[s, :, columns] = fin[tab[T_F + s]]

    @pl.loop(0, NC + 4)
    def _(n):
        @pl.when(n < NC)
        def _():
            hand_copy(n).wait_recv()

            @pl.when(n + 3 < NC)
            def _():
                phase1(n + 3)

            @pl.when(n + 2 < NC)
            def _():
                phase2(n + 2)

            compute(n)

            @pl.when(n + 1 < NC)
            def _():
                hand_over(n + 1)

            send_first(n)

        for h in (1, 2, 3, 4):
            @pl.when((n - h >= 0) & (n - h < NC))
            def _():
                forward(n - h, h)
                if h == 4:
                    assemble(n - h)

    pair_copy.wait_send()
    for k in range(NZ - 1):
        z_copy(k).wait_send()

    @pl.loop(0, NC)
    def _(n):
        for k in range(np1):
            p1_copy(n, k).wait_send()
        for j in range(np1 + 1):
            for l in range(np2):
                p2_copy(n, j, l).wait_send()
        hand_copy(n).wait_send()
        pair_block_copy(n).wait_send()
        for h in range(4):
            hop_a(n, h).wait_send()
        for h in range(3):
            hop_b(n, h).wait_send()


def rotary(rows):
    m = np.arange(HD // 2, dtype=np.float64)
    angle = np.arange(rows, dtype=np.float64)[:, None] * (1000000.0 ** (-2.0 * m / HD))[None, :]
    cos, sin = np.cos(angle), np.sin(angle)
    return np.stack([np.concatenate([cos, cos], 1), np.concatenate([-sin, sin], 1)]).astype(np.float32)


def local(ny, nx, hidden, lengths, kv_weight, input_gain, key_gain):
    rows, depth = hidden.shape
    piece = depth // (ny * nx)
    g, t = lax.axis_index("grp"), lax.axis_index("tp")
    vm, sm, anym = (pl.BlockSpec(memory_space=s) for s in (pltpu.VMEM, pltpu.SMEM, pl.ANY))
    tab = pl.pallas_call(
        table_kernel,
        out_shape=jax.ShapeDtypeStruct((T_SIZE,), I32),
        in_specs=[sm],
        out_specs=sm,
        scratch_shapes=[pltpu.SMEM((2 * NZ + 1,), I32)],
        name="tables",
    )(lengths)
    gain = lax.dynamic_slice(input_gain, (g * piece,), (piece,))
    scaled = (kv_weight.astype(F32) * gain[:, None]).astype(BF)
    lane = lax.broadcasted_iota(I32, (piece, HD), 1) // (HD // 2)
    wp = jnp.where(lane == t % 2, jnp.concatenate([scaled, scaled], axis=1), jnp.zeros((), BF))
    blk = lambda *s: pltpu.VMEM((*s, BLK, HD), BF)
    dma = lambda *s: pltpu.SemaphoreType.DMA(s)
    half = piece // 2
    return pl.pallas_call(
        functools.partial(main_kernel, ny, nx, rows, depth),
        out_shape=jax.ShapeDtypeStruct((PAGES, BLK, NC * HD), BF),
        in_specs=[sm, vm, vm, anym, anym],
        out_specs=vm,
        scratch_shapes=[
            pltpu.VMEM((rows, depth), BF),
            pltpu.VMEM((2, rows, HD), F32),
            pltpu.VMEM((rows, HD), F32),
            pltpu.VMEM((NC, ny, nx, 2, half, HD), BF),
            pltpu.VMEM((half, HD), BF),
            blk(NB),
            pltpu.VMEM((3 * BLK, HD), F32),
            blk(NC, SRC),
            blk(ZERO + 1),
            blk(NC, 5),
            blk(NC, 5),
            blk(NC, CA[0]),
            blk(NC, CB[0]),
            *[blk(NC, s) for s in CA],
            *[blk(NC, s) for s in CB],
            dma(NB),
            pltpu.SemaphoreType.DMA,
            pltpu.SemaphoreType.DMA,
            pltpu.SemaphoreType.DMA,
            dma(NZ - 1),
            dma(NC),
            dma(NC, max(nx - 1, 1)),
            dma(NC, max(nx - 1, 1)),
            dma(NC, nx, max(ny - 1, 1)),
            dma(NC),
            dma(NC),
            dma(NC),
            dma(NC, 8),
            dma(NC, 8),
        ],
        compiler_params=pltpu.CompilerParams(
            collective_id=0, has_side_effects=True, vmem_limit_bytes=66_000_000
        ),
        name="recompute",
    )(tab, wp, key_gain[None, :], jnp.asarray(rotary(rows)), hidden)


def solution(mesh):
    side = math.isqrt(mesh.shape["grp"])
    placed = (P(("grp", "tp"), None), P("grp", None), P("grp", "tp"), P(), P())
    return jax.shard_map(
        functools.partial(local, side, side),
        mesh=mesh,
        in_specs=placed,
        out_specs=P(("grp", "tp"), None, None),
        check_vma=False,
    )
```

time: 250 us -> 128 us (0.51)
  waiting for transfers between devices: 148 us -> 0 us
  Pallas kernels: 0 us -> 123 us
  other arithmetic: 29.7 us -> 0.85 us
  blocking collectives: 20.4 us -> 0 us
  matrix products: 16.9 us -> 0 us
  between operations: 13.6 us -> 0.04 us
  local copies, waits for them, and re-layouts: 16.5 us -> 4.19 us
  starting transfers between devices: 4.66 us -> 0 us
    pallas_call x0 -> x2, Pallas kernels: none -> 123 us  [the longest x1 121 us: local(): pl.pallas_call(functools.partial(main_kernel, ny, nx, rows, depth), out_s...]
    all_to_all x1 -> x0, waiting for transfers between devices: 91.5 us -> none  [local(): lax.all_to_all(outgoing, 'tp', split_axis=0, concat_axis=0, tiled=True)]
    all_gather x1 -> x0, waiting for transfers between devices: 56.4 us -> none  [project(): lax.all_gather(all_rows, 'tp', axis=1, tiled=True)]
    all_gather x1 -> x0, blocking collectives: 20.4 us -> none  [project(): all_rows = lax.all_gather(kv_weight, 'grp', axis=0, tiled=True)]
    dot_general x1 -> x0, matrix products: 16.9 us -> none  [project(): jnp.dot(normed, lax.all_gather(all_rows, 'tp', axis=1, tiled=True), prefe...]
    reduce_sum x3 -> x0, other arithmetic: 8.91 us -> none  [the longest x1 6.71 us: normalize(): jnp.mean(values * values, axis=-1, keepdims=True) + norm_eps]
    gather x3 -> x0, local copies, waits for them, and re-layouts: 6.33 us -> none  [the longest x1 2.87 us: local(): jnp.take(own_cache, picked_local, axis=0)]
    select_n x6 -> x1, other arithmetic: 6.6 us -> 0.73 us  [local(): jnp.where(lane == t % 2, jnp.concatenate([scaled, scaled], axis=1), jnp.z...]
  transfers between devices with their start and end apart: 2 -> 0, of which waited for: 2 -> 0; matrix products, arithmetic and copies ran while one was open for 7% -> 0% of each run, Pallas kernels for 0% -> 0%
where the time goes in v1:
time: 128 us
  Pallas kernels  123 us (96%)
  local copies, waits for them, and re-layouts  4.19 us (3%)
    pallas_call x1, Pallas kernels, local(): pl.pallas_call(functools.partial(main_kernel, ny, nx, rows, depth), out_s...  121 us

profile of v1, /device:TPU:1, one launch (start us, length us, event | category | flops | bytes accessed | tf_op | source)
XLA Modules:
  0.0 127.8 jit_solution(1802734799394733706)
XLA Ops:
  0.0 1.6 %tables.1.refs_0_ = s32[32]{0:T(128)} custom-call(s32[1,16]{1,0:T(1,128)} %len_ref.1), custom_call_target="tpu_custom_call" | custom-call | tf_op jit(solution)/shard_map/tables/pallas_call | solution.py:379
  1.7 0.8 dynamic_slice.3
  2.4 0.9 copy.8
  3.3 0.1 multiply_convert_fusion
  3.4 0.7 fusion.refs_1_
  4.2 121.1 %recompute.1 = bf16[5,128,1024]{2,1,0:T(8,128)(2,1)} custom-call(s32[32]{0:T(128)} %tables.1.refs_0_, bf16[320,128]{1,0:T(8,128)(2,1)} %fusion.refs_1_, f32[1,128]{1,0:T(1,128)} %bitcast.1, f32[2,1152,128]{2,1,0:T(8,128)} %constant.47.clone.refs_3_, bf16[1152,5120]{1,0:T(8,128)(2,1)} %refs_4_.1), custom_call_target="tpu_custom_call" | custom-call | tf_op jit(solution)/shard_map/recompute/pallas_call | solution.py:394
  125.3 2.5 %copy.10 = bf16[5,128,1024]{2,1,0:T(8,128)(2,1)} copy(bf16[5,128,1024]{2,1,0:T(8,128)(2,1)} %recompute.1) | data formatting | bytes 2621440
  (2 shorter events, 0.0 us)

commit v2 on v1

v2 whole, which is shorter than its diff:
```python
import functools
import math

import jax
import jax.numpy as jnp
import numpy as np
from jax import lax
from jax.experimental import pallas as pl
from jax.experimental.pallas import tpu as pltpu
from jax.sharding import PartitionSpec as P

HD = 128
BLK = 128
NB = 9
NZ = 8
PAGES = 5
NC = 4
CW = 256
EPS = 1e-06
MESH = pl.DeviceIdType.MESH
BF, F32, I32 = jnp.bfloat16, jnp.float32, jnp.int32

CA = (5, 4, 3, 2)
CB = (4, 3, 2)
SRC = 10
BASE_A = tuple(SRC + sum(CA[:i]) for i in range(4))
BASE_B = tuple(SRC + sum(CA) + sum(CB[:i]) for i in range(3))
ZERO = SRC + sum(CA) + sum(CB)
NS = ZERO + 1
T_LEN, T_P, T_O, T_A, T_B, T_F, T_J = 0, 1, 6, 11, 16, 20, 25
T_SIZE = 32


def tables(first, length, z, c, where):
    d = 1 - 2 * c
    seq = 2 * z + c

    def begin(zz):
        return (first(2 * zz) - c + 1) >> 1

    out = {T_LEN: length}
    fs = first(seq)
    for e in range(5):
        b = ((fs + 1 - c) & 1) + 2 * e
        out[T_P + e] = where(b > NB - 1, NB - 1, b)
        b = ((fs + c) & 1) + 2 * e
        out[T_O + e] = where(b > NB - 1, NB - 1, b)
    m0, m1 = begin(z), begin(z + 1)
    q0 = ((first(2 * z + 1) - c + 1) >> 1) - m0

    def source_index(u):
        lead = u < q0
        v = where(c == 0, where(lead, u, 5 + u - q0), where(lead, 5 + u, u - q0))
        v = where(v < 0, 0, v)
        return where(v > SRC - 1, SRC - 1, v)

    for base, slots, order in ((T_A, CA[0], (4, 3, 2, 1)), (T_B, CB[0], (5, 6, 7))):
        pos = 0
        table = [0] * slots
        for kap in order:
            first_m = m0 + ((z + d * kap - m0) & 7)
            for e in range(2):
                m = first_m + 8 * e
                present = m < m1
                value = source_index(m - m0)
                for q in range(slots):
                    table[q] = where(present & (pos == q), value, table[q])
                pos = pos + where(present, 1, 0)
        for q in range(slots):
            out[base + q] = table[q]
    total = first(2 * NZ)
    begins = [begin(i) for i in range(NZ + 1)]
    for s in range(PAGES):
        m = 8 * s + z
        zs = 0
        for i in range(NZ - 1):
            zs = zs + where(begins[i + 1] <= m, 1, 0)
        s0, s1 = begins[0], begins[1]
        for i in range(1, NZ):
            s0 = where(zs == i, begins[i], s0)
            s1 = where(zs == i, begins[i + 1], s1)
        kap = (d * (z - zs)) & 7
        second = where(m - 8 >= s0, 1, 0)

        def count(k):
            f = s0 + ((zs + d * k - s0) & 7)
            return where(f < s1, 1, 0) + where(f + 8 < s1, 1, 0)

        value = source_index(m - m0)
        pos = second
        for k in (4, 3, 2, 1):
            value = where(kap == k, BASE_A[k - 1] + pos, value)
            pos = pos + count(k)
        pos = second
        for k in (5, 6, 7):
            value = where(kap == k, BASE_B[7 - k] + pos, value)
            pos = pos + count(k)
        out[T_J + s] = zs >> 1
        out[T_F + s] = where(16 * s + 2 * z + c < total, value, ZERO)
    return out


def table_kernel(len_ref, tab_ref, first_ref):
    t = lax.axis_index("tp")
    z, c = t // 2, t % 2
    running = jnp.int32(0)
    first_ref[0] = running
    for i in range(2 * NZ):
        running = running + ((len_ref[0, i] + (BLK - 1)) >> 7)
        first_ref[i + 1] = running
    out = tables(lambda i: first_ref[i], len_ref[0, t], z, c, jnp.where)
    for i in range(T_SIZE):
        tab_ref[i] = jnp.asarray(out.get(i, 0), I32)


def main_kernel(rows, depth, *refs):
    (tab, wp, kg, cs_hbm, x_hbm, out,
     xv, csv, rs, W, pairb, own, acc, fin, stp, prv, sta, stb,
     ra1, ra2, ra3, ra4, rb1, rb2, rb3,
     x_sem, cs_sem, pair_s, pair_r, z_s, z_r,
     p1_s, p1_r, p1h_s, p1h_r, p2_s, p2_r, p2h_s, p2h_r, h_s, h_r, a2a_s, a2a_r) = refs
    ra, rb = (ra1, ra2, ra3, ra4), (rb1, rb2, rb3)
    half = depth // 32
    quarter = half // 2
    g, t = lax.axis_index("grp"), lax.axis_index("tp")
    z, c = t // 2, t % 2
    y, x = g // 4, g % 4
    d = 1 - 2 * c
    zp = z // 2

    def dev(gg, tt):
        return {"grp": gg, "tp": tt}

    partner = dev(g, t + d)
    z_peers = [dev(g, 2 * (2 * zp + (1 - z % 2)) + c)]
    for k in (1, 2, 3):
        for e in (0, 1):
            z_peers.append(dev(g, 2 * (2 * ((zp + 4 - k) % 4) + e) + c))
    far = dev(g, 2 * ((z + d + NZ) % NZ) + c)
    near = dev(g, 2 * ((z - d + NZ) % NZ) + c)

    def at(a, b):
        yy = (y + jnp.where(c == 0, b, a) + 4) % 4
        xx = (x + jnp.where(c == 0, a, b) + 4) % 4
        return yy, xx

    def peer(a, b):
        yy, xx = at(a, b)
        return dev(yy * 4 + xx, t)

    first = (peer(1, 0), peer(-1, 0))
    second = (peer(0, 1), peer(0, -1))
    offsets = (0, -1, 1, 2)

    def x_copy(b):
        rows_b = pl.ds(pl.multiple_of(b * BLK, BLK), BLK)
        return pltpu.make_async_copy(x_hbm.at[rows_b], xv.at[rows_b], x_sem.at[b])

    cs_copy = pltpu.make_async_copy(cs_hbm, csv, cs_sem)

    @pl.loop(0, NB)
    def _(b):
        x_copy(b).start()

    cs_copy.start()

    barrier = pltpu.get_barrier_semaphore()
    everyone = [partner, *z_peers, *first, *second]
    for p in everyone:
        pl.semaphore_signal(barrier, inc=1, device_id=p, device_id_type=MESH)
    pl.semaphore_wait(barrier, len(everyone))

    def remote(s, r, ss, rr, p):
        return pltpu.make_async_remote_copy(
            src_ref=s, dst_ref=r, send_sem=ss, recv_sem=rr, device_id=p, device_id_type=MESH
        )

    def arrived(ref, sem):
        pltpu.make_async_copy(ref, ref, sem).wait()

    pair_copy = remote(
        wp.at[pl.ds(pl.multiple_of((1 - c) * half, half), half)], pairb, pair_s, pair_r, partner
    )
    pair_copy.start()
    pair_copy.wait_recv()
    mine = wp[pl.ds(pl.multiple_of(c * half, half), half)]
    W[z, y, x, c] = mine + pairb[...]

    def z_copy(k):
        return remote(W.at[z, y, x, c], W.at[z, y, x, c], z_s.at[k], z_r.at[z], z_peers[k])

    for k in range(NZ - 1):
        z_copy(k).start()

    def chunk(s):
        return (zp + s) % NC

    def piece(s, a, b):
        yy, xx = at(a, b)
        return W.at[pl.ds(2 * chunk(s), 2), yy, xx, c]

    def part(s, a, b, h):
        yy, xx = at(a, b)
        return W.at[pl.ds(2 * chunk(s), 2), yy, xx, c, pl.ds(h * quarter, quarter)]

    def p1_copy(s, v):
        return remote(piece(s, 0, 0), piece(s, 0, 0), p1_s.at[s, v], p1_r.at[s, v], first[v])

    def p1h_copy(s, v):
        w = part(s, -1 if v == 0 else 1, 0, v)
        return remote(w, w, p1h_s.at[s, v], p1h_r.at[s, v], first[v])

    def p2_copy(s, v, i):
        w = piece(s, offsets[i], 0)
        return remote(w, w, p2_s.at[s, v, i], p2_r.at[s, v, i], second[v])

    def p2h_copy(s, v, i):
        w = part(s, offsets[i], -1 if v == 0 else 1, v)
        return remote(w, w, p2h_s.at[s, v, i], p2h_r.at[s, v], second[v])

    def hand_copy(s, i, j):
        w = piece(s, offsets[i], offsets[j])
        return remote(w, w, h_s.at[s, i, j], h_r.at[s], partner)

    one = W.at[pl.ds(0, 2), 0, 0, 0]
    one_part = W.at[pl.ds(0, 2), 0, 0, 0, pl.ds(0, quarter)]
    four_parts = W.at[pl.ds(0, 2), 0, :, 0, pl.ds(0, quarter)]
    whole_half = W.at[pl.ds(0, 2), :, :, 0]

    def send_row(s, i):
        for v in range(2):
            p2_copy(s, v, i).start()
        hand_copy(s, i, 0).start()

    def stage1(s, own_pair):
        if own_pair:
            arrived(W.at[0, 0, 0, 0], z_r.at[2 * zp + (1 - z % 2)])
        else:
            for e in range(2):
                arrived(W.at[0, 0, 0, 0], z_r.at[2 * chunk(s) + e])
        for v in range(2):
            p1_copy(s, v).start()
        send_row(s, 0)

    def stage2(s):
        for v in range(2):
            arrived(one, p1_r.at[s, v])
            p1h_copy(s, v).start()
            send_row(s, 1 + v)

    def stage3(s):
        for v in range(2):
            arrived(one_part, p1h_r.at[s, v])
        send_row(s, 3)
        for i in range(4):
            for v in range(2):
                arrived(one, p2_r.at[s, v, i])
                p2h_copy(s, v, i).start()
                hand_copy(s, i, 1 + v).start()

    def stage4(s):
        for v in range(2):
            arrived(four_parts, p2h_r.at[s, v])
        for i in range(4):
            hand_copy(s, i, 3).start()

    length = tab[T_LEN]

    def row_scales(lo, hi):
        @pl.loop(lo, hi)
        def _(b):
            x_copy(b).wait()
            r0 = pl.multiple_of(b * BLK, BLK)
            rows_b = pl.ds(r0, BLK)
            total = jnp.zeros((BLK, HD), F32)
            for k in range(depth // HD):
                v = xv[rows_b, k * HD:(k + 1) * HD].astype(F32)
                total = total + v * v
            mean = jnp.sum(total, axis=1, keepdims=True) * (1.0 / depth)
            scale = jnp.broadcast_to(lax.rsqrt(mean + EPS), (BLK, HD))
            p = r0 + lax.broadcasted_iota(I32, (BLK, HD), 0)
            rs[rows_b, :] = jnp.where(p < length, scale, 0.0)

    stage1(0, True)
    row_scales(0, 2)
    stage2(0)
    row_scales(2, 4)
    stage3(0)
    stage1(1, False)
    row_scales(4, 7)
    stage4(0)
    stage2(1)
    row_scales(7, NB)
    cs_copy.wait()
    for j in range(NC):
        fin[j * NS + ZERO] = jnp.zeros((BLK, CW), BF)

    def compute(j):
        n = chunk(j)
        tile = 3 * BLK

        @pl.loop(0, NB // 3)
        def _(i):
            r0 = pl.multiple_of(i * tile, tile)
            rows_i = pl.ds(r0, tile)
            w = jnp.concatenate(
                [W[2 * n].reshape(depth, HD), W[2 * n + 1].reshape(depth, HD)], axis=1
            )
            a = jnp.dot(xv[rows_i, :], w, preferred_element_type=F32)
            scale = rs[rows_i, :]
            acc[...] = a * jnp.concatenate([scale, scale], axis=1)

            @pl.when(n < NC // 2)
            def _():
                for h in range(2):
                    k = acc[:, h * HD:(h + 1) * HD]
                    s = lax.rsqrt(jnp.mean(k * k, axis=1, keepdims=True) + EPS)
                    k = k * s * kg[...]
                    turned = k * csv[0, rows_i, :] + pltpu.roll(k, HD // 2, 1) * csv[1, rows_i, :]
                    own[pl.ds(3 * i, 3), :, h * HD:(h + 1) * HD] = turned.astype(BF).reshape(3, BLK, HD)

            @pl.when(n >= NC // 2)
            def _():
                own[pl.ds(3 * i, 3)] = acc[...].astype(BF).reshape(3, BLK, CW)

    def pair_block_copy(j):
        return remote(stp.at[j], prv.at[j], a2a_s.at[j, 0], a2a_r.at[j, 0], partner)

    def hop_a(j, h):
        s = sta.at[j] if h == 0 else ra[h - 1].at[j, pl.ds(0, CA[h])]
        return remote(s, ra[h].at[j], a2a_s.at[j, 1 + h], a2a_r.at[j, 1 + h], far)

    def hop_b(j, h):
        s = stb.at[j] if h == 0 else rb[h - 1].at[j, pl.ds(0, CB[h])]
        return remote(s, rb[h].at[j], a2a_s.at[j, 5 + h], a2a_r.at[j, 5 + h], near)

    def send_first(j):
        base = j * NS
        for e in range(5):
            stp[j, e] = own[tab[T_P + e]]
        pair_block_copy(j).start()
        for e in range(5):
            fin[base + e] = own[tab[T_O + e]]
        pair_block_copy(j).wait_recv()
        for e in range(5):
            fin[base + 5 + e] = prv[j, e]
        for q in range(CA[0]):
            sta[j, q] = fin[base + tab[T_A + q]]
        hop_a(j, 0).start()
        for q in range(CB[0]):
            stb[j, q] = fin[base + tab[T_B + q]]
        hop_b(j, 0).start()

    def forward(j, h):
        hop_a(j, h - 1).wait_recv()
        if h < 4:
            hop_a(j, h).start()
        if h < 4:
            hop_b(j, h - 1).wait_recv()
        if h < 3:
            hop_b(j, h).start()
        base = j * NS
        for q in range(CA[h - 1]):
            fin[base + BASE_A[h - 1] + q] = ra[h - 1][j, q]
        if h < 4:
            for q in range(CB[h - 1]):
                fin[base + BASE_B[h - 1] + q] = rb[h - 1][j, q]

    @pl.loop(0, NC + 4)
    def _(j):
        @pl.when(j < NC)
        def _():
            arrived(whole_half, h_r.at[j])

            @pl.when(j + 2 < NC)
            def _():
                stage1(j + 2, False)

            compute(j)

            @pl.when(j + 1 < NC)
            def _():
                stage3(j + 1)

            send_first(j)

            @pl.when(j + 2 < NC)
            def _():
                stage2(j + 2)

        for h in (1, 2, 3, 4):
            @pl.when((j - h >= 0) & (j - h < NC))
            def _():
                forward(j - h, h)

        @pl.when(j + 1 < NC)
        def _():
            stage4(j + 1)

    for s in range(PAGES):
        slot, pair = tab[T_F + s], tab[T_J + s]
        for n in range(NC):
            out[s, :, n * CW:(n + 1) * CW] = fin[((n + NC - pair) % NC) * NS + slot]

    pair_copy.wait_send()
    for k in range(NZ - 1):
        z_copy(k).wait_send()

    @pl.loop(0, NC)
    def _(s):
        for v in range(2):
            p1_copy(s, v).wait_send()
            p1h_copy(s, v).wait_send()
            for i in range(4):
                p2_copy(s, v, i).wait_send()
                p2h_copy(s, v, i).wait_send()
        for i in range(4):
            for j in range(4):
                hand_copy(s, i, j).wait_send()
        pair_block_copy(s).wait_send()
        for h in range(4):
            hop_a(s, h).wait_send()
        for h in range(3):
            hop_b(s, h).wait_send()


def rotary(rows):
    m = np.arange(HD // 2, dtype=np.float64)
    angle = np.arange(rows, dtype=np.float64)[:, None] * (1000000.0 ** (-2.0 * m / HD))[None, :]
    cos, sin = np.cos(angle), np.sin(angle)
    return np.stack([np.concatenate([cos, cos], 1), np.concatenate([-sin, sin], 1)]).astype(np.float32)


def local(hidden, lengths, kv_weight, input_gain, key_gain):
    rows, depth = hidden.shape
    piece = depth // 16
    g, t = lax.axis_index("grp"), lax.axis_index("tp")
    vm, sm, anym = (pl.BlockSpec(memory_space=s) for s in (pltpu.VMEM, pltpu.SMEM, pl.ANY))
    tab = pl.pallas_call(
        table_kernel,
        out_shape=jax.ShapeDtypeStruct((T_SIZE,), I32),
        in_specs=[sm],
        out_specs=sm,
        scratch_shapes=[pltpu.SMEM((2 * NZ + 1,), I32)],
        name="tables",
    )(lengths)
    gain = lax.dynamic_slice(input_gain, (g * piece,), (piece,))
    scaled = (kv_weight.astype(F32) * gain[:, None]).astype(BF)
    lane = lax.broadcasted_iota(I32, (piece, HD), 1) // (HD // 2)
    wp = jnp.where(lane == t % 2, jnp.concatenate([scaled, scaled], axis=1), jnp.zeros((), BF))
    blk = lambda *s: pltpu.VMEM((*s, BLK, CW), BF)
    dma = lambda *s: pltpu.SemaphoreType.DMA(s)
    half = piece // 2
    return pl.pallas_call(
        functools.partial(main_kernel, rows, depth),
        out_shape=jax.ShapeDtypeStruct((PAGES, BLK, NC * CW), BF),
        in_specs=[sm, vm, vm, anym, anym],
        out_specs=vm,
        scratch_shapes=[
            pltpu.VMEM((rows, depth), BF),
            pltpu.VMEM((2, rows, HD), F32),
            pltpu.VMEM((rows, HD), F32),
            pltpu.VMEM((NZ, 4, 4, 2, half, HD), BF),
            pltpu.VMEM((half, HD), BF),
            blk(NB),
            pltpu.VMEM((3 * BLK, CW), F32),
            blk(NC * NS),
            blk(NC, 5),
            blk(NC, 5),
            blk(NC, CA[0]),
            blk(NC, CB[0]),
            *[blk(NC, s) for s in CA],
            *[blk(NC, s) for s in CB],
            dma(NB),
            *[pltpu.SemaphoreType.DMA] * 3,
            dma(NZ - 1),
            dma(NZ),
            *[dma(NC, 2)] * 4,
            *[dma(NC, 2, 4)] * 3,
            dma(NC, 2),
            dma(NC, 4, 4),
            dma(NC),
            dma(NC, 8),
            dma(NC, 8),
        ],
        compiler_params=pltpu.CompilerParams(
            collective_id=0, has_side_effects=True, vmem_limit_bytes=66_000_000
        ),
        name="recompute",
    )(tab, wp, key_gain[None, :], jnp.asarray(rotary(rows)), hidden)


def solution(mesh):
    placed = (P(("grp", "tp"), None), P("grp", None), P("grp", "tp"), P(), P())
    return jax.shard_map(
        local,
        mesh=mesh,
        in_specs=placed,
        out_specs=P(("grp", "tp"), None, None),
        check_vma=False,
    )
```

time: 128 us -> 128 us (level)
  no operation moved by 1% of the time
where the time goes in v2:
time: 128 us
  Pallas kernels  123 us (96%)
  local copies, waits for them, and re-layouts  4.19 us (3%)
    pallas_call x1, Pallas kernels, local(): pl.pallas_call(functools.partial(main_kernel, rows, depth), out_shape=jax...  121 us

profile of v2, /device:TPU:1, one launch (start us, length us, event | category | flops | bytes accessed | tf_op | source)
XLA Modules:
  0.0 128.2 jit_solution(3658273460109358625)
XLA Ops:
  0.0 1.6 %tables.1.refs_0_ = s32[32]{0:T(128)} custom-call(s32[1,16]{1,0:T(1,128)} %len_ref.1), custom_call_target="tpu_custom_call" | custom-call | tf_op jit(solution)/shard_map/tables/pallas_call | solution.py:439
  1.7 0.8 dynamic_slice.3
  2.4 0.9 copy.8
  3.3 0.1 multiply_convert_fusion
  3.5 0.7 fusion.refs_1_
  4.2 121.5 %recompute.1 = bf16[5,128,1024]{2,1,0:T(8,128)(2,1)} custom-call(s32[32]{0:T(128)} %tables.1.refs_0_, bf16[320,128]{1,0:T(8,128)(2,1)} %fusion.refs_1_, f32[1,128]{1,0:T(1,128)} %bitcast.1, f32[2,1152,128]{2,1,0:T(8,128)} %constant.47.clone.refs_3_, bf16[1152,5120]{1,0:T(8,128)(2,1)} %refs_4_.1), custom_call_target="tpu_custom_call" | custom-call | tf_op jit(solution)/shard_map/recompute/pallas_call | solution.py:454
  125.7 2.5 %copy.10 = bf16[5,128,1024]{2,1,0:T(8,128)(2,1)} copy(bf16[5,128,1024]{2,1,0:T(8,128)(2,1)} %recompute.1) | data formatting | bytes 2621440
  (2 shorter events, 0.0 us)

commit v3 on v2

--- a/solution.py
+++ b/solution.py
@@ -14,8 +14,8 @@
 NB = 9
 NZ = 8
 PAGES = 5
-NC = 4
-CW = 256
+NC = 8
+CW = 128
 EPS = 1e-06
 MESH = pl.DeviceIdType.MESH
 BF, F32, I32 = jnp.bfloat16, jnp.float32, jnp.int32
@@ -95,7 +95,7 @@
         for k in (5, 6, 7):
             value = where(kap == k, BASE_B[7 - k] + pos, value)
             pos = pos + count(k)
-        out[T_J + s] = zs >> 1
+        out[T_J + s] = zs
         out[T_F + s] = where(16 * s + 2 * z + c < total, value, ZERO)
     return out
 
@@ -114,8 +114,8 @@
 
 
 def main_kernel(rows, depth, *refs):
-    (tab, wp, kg, cs_hbm, x_hbm, out,
-     xv, csv, rs, W, pairb, own, acc, fin, stp, prv, sta, stb,
+    (tab, wt, gain, kg, cs_hbm, x_hbm, out,
+     xv, csv, rs, W, turn, wp, pairb, own, acc, fin, stp, prv, sta, stb,
      ra1, ra2, ra3, ra4, rb1, rb2, rb3,
      x_sem, cs_sem, pair_s, pair_r, z_s, z_r,
      p1_s, p1_r, p1h_s, p1h_r, p2_s, p2_r, p2h_s, p2h_r, h_s, h_r, a2a_s, a2a_r) = refs
@@ -126,16 +126,12 @@
     z, c = t // 2, t % 2
     y, x = g // 4, g % 4
     d = 1 - 2 * c
-    zp = z // 2
 
     def dev(gg, tt):
         return {"grp": gg, "tp": tt}
 
     partner = dev(g, t + d)
-    z_peers = [dev(g, 2 * (2 * zp + (1 - z % 2)) + c)]
-    for k in (1, 2, 3):
-        for e in (0, 1):
-            z_peers.append(dev(g, 2 * (2 * ((zp + 4 - k) % 4) + e) + c))
+    above, below = dev(g, 2 * ((z + 1) % NZ) + c), dev(g, 2 * ((z + NZ - 1) % NZ) + c)
     far = dev(g, 2 * ((z + d + NZ) % NZ) + c)
     near = dev(g, 2 * ((z - d + NZ) % NZ) + c)
 
@@ -165,9 +161,19 @@
     cs_copy.start()
 
     barrier = pltpu.get_barrier_semaphore()
-    everyone = [partner, *z_peers, *first, *second]
+    everyone = [partner, above, below, *first, *second]
     for p in everyone:
         pl.semaphore_signal(barrier, inc=1, device_id=p, device_id_type=MESH)
+
+    piece_k = depth // 16
+    odd = (g * piece_k) % HD
+    window = gain[:, pl.ds(pl.multiple_of(g * piece_k - odd, HD), piece_k + HD // 2)]
+    window = jnp.where(odd == 0, window, pltpu.roll(window, piece_k, 1))
+    turn[...] = jnp.zeros_like(turn)
+    scaled = wt[...].astype(F32) * window[:, :piece_k]
+    turn[pl.ds(pl.multiple_of(c * (HD // 2), HD // 2), HD // 2), :piece_k] = scaled
+    wp[...] = turn[...].T[:piece_k].astype(BF)
+
     pl.semaphore_wait(barrier, len(everyone))
 
     def remote(s, r, ss, rr, p):
@@ -186,22 +192,16 @@
     mine = wp[pl.ds(pl.multiple_of(c * half, half), half)]
     W[z, y, x, c] = mine + pairb[...]
 
-    def z_copy(k):
-        return remote(W.at[z, y, x, c], W.at[z, y, x, c], z_s.at[k], z_r.at[z], z_peers[k])
-
-    for k in range(NZ - 1):
-        z_copy(k).start()
-
-    def chunk(s):
-        return (zp + s) % NC
+    def unit(s):
+        return (z + jnp.where(s % 2 == 1, (s + 1) // 2, NZ - s // 2)) % NZ
 
     def piece(s, a, b):
         yy, xx = at(a, b)
-        return W.at[pl.ds(2 * chunk(s), 2), yy, xx, c]
+        return W.at[unit(s), yy, xx, c]
 
     def part(s, a, b, h):
         yy, xx = at(a, b)
-        return W.at[pl.ds(2 * chunk(s), 2), yy, xx, c, pl.ds(h * quarter, quarter)]
+        return W.at[unit(s), yy, xx, c, pl.ds(h * quarter, quarter)]
 
     def p1_copy(s, v):
         return remote(piece(s, 0, 0), piece(s, 0, 0), p1_s.at[s, v], p1_r.at[s, v], first[v])
@@ -222,25 +222,37 @@
         w = piece(s, offsets[i], offsets[j])
         return remote(w, w, h_s.at[s, i, j], h_r.at[s], partner)
 
-    one = W.at[pl.ds(0, 2), 0, 0, 0]
-    one_part = W.at[pl.ds(0, 2), 0, 0, 0, pl.ds(0, quarter)]
-    four_parts = W.at[pl.ds(0, 2), 0, :, 0, pl.ds(0, quarter)]
-    whole_half = W.at[pl.ds(0, 2), :, :, 0]
+    one = W.at[0, 0, 0, 0]
+    one_part = W.at[0, 0, 0, 0, pl.ds(0, quarter)]
+    four_parts = W.at[0, 0, :, 0, pl.ds(0, quarter)]
+    whole_half = W.at[0, :, :, 0]
 
     def send_row(s, i):
         for v in range(2):
             p2_copy(s, v, i).start()
         hand_copy(s, i, 0).start()
 
-    def stage1(s, own_pair):
-        if own_pair:
-            arrived(W.at[0, 0, 0, 0], z_r.at[2 * zp + (1 - z % 2)])
-        else:
-            for e in range(2):
-                arrived(W.at[0, 0, 0, 0], z_r.at[2 * chunk(s) + e])
+    def z_pass(s, to, up):
+        w = W.at[unit(s), y, x, c]
+        return remote(w, w, z_s.at[to], z_r.at[to], above if up else below)
+
+    def stage1(s):
         for v in range(2):
             p1_copy(s, v).start()
         send_row(s, 0)
+
+    def z_step(s):
+        arrived(one, z_r.at[s])
+
+        @pl.when((s % 2 == 1) & (s + 2 < NC))
+        def _():
+            z_pass(s, s + 2, False).start()
+
+        @pl.when((s % 2 == 0) & (s + 2 < NC))
+        def _():
+            z_pass(s, s + 2, True).start()
+
+        stage1(s)
 
     def stage2(s):
         for v in range(2):
@@ -281,43 +293,40 @@
             p = r0 + lax.broadcasted_iota(I32, (BLK, HD), 0)
             rs[rows_b, :] = jnp.where(p < length, scale, 0.0)
 
-    stage1(0, True)
+    z_pass(0, 1, False).start()
+    z_pass(0, 2, True).start()
+    stage1(0)
     row_scales(0, 2)
     stage2(0)
     row_scales(2, 4)
     stage3(0)
-    stage1(1, False)
-    row_scales(4, 7)
+    z_step(1)
+    row_scales(4, 6)
     stage4(0)
     stage2(1)
-    row_scales(7, NB)
+    row_scales(6, NB)
     cs_copy.wait()
     for j in range(NC):
         fin[j * NS + ZERO] = jnp.zeros((BLK, CW), BF)
 
     def compute(j):
-        n = chunk(j)
+        n = unit(j)
         tile = 3 * BLK
 
         @pl.loop(0, NB // 3)
         def _(i):
             r0 = pl.multiple_of(i * tile, tile)
             rows_i = pl.ds(r0, tile)
-            w = jnp.concatenate(
-                [W[2 * n].reshape(depth, HD), W[2 * n + 1].reshape(depth, HD)], axis=1
-            )
-            a = jnp.dot(xv[rows_i, :], w, preferred_element_type=F32)
-            scale = rs[rows_i, :]
-            acc[...] = a * jnp.concatenate([scale, scale], axis=1)
+            a = jnp.dot(xv[rows_i, :], W[n].reshape(depth, HD), preferred_element_type=F32)
+            acc[...] = a * rs[rows_i, :]
 
             @pl.when(n < NC // 2)
             def _():
-                for h in range(2):
-                    k = acc[:, h * HD:(h + 1) * HD]
-                    s = lax.rsqrt(jnp.mean(k * k, axis=1, keepdims=True) + EPS)
-                    k = k * s * kg[...]
-                    turned = k * csv[0, rows_i, :] + pltpu.roll(k, HD // 2, 1) * csv[1, rows_i, :]
-                    own[pl.ds(3 * i, 3), :, h * HD:(h + 1) * HD] = turned.astype(BF).reshape(3, BLK, HD)
+                k = acc[...]
+                s = lax.rsqrt(jnp.mean(k * k, axis=1, keepdims=True) + EPS)
+                k = k * s * kg[...]
+                turned = k * csv[0, rows_i, :] + pltpu.roll(k, HD // 2, 1) * csv[1, rows_i, :]
+                own[pl.ds(3 * i, 3)] = turned.astype(BF).reshape(3, BLK, HD)
 
             @pl.when(n >= NC // 2)
             def _():
@@ -374,15 +383,14 @@
 
             @pl.when(j + 2 < NC)
             def _():
-                stage1(j + 2, False)
+                z_step(j + 2)
 
             compute(j)
+            send_first(j)
 
             @pl.when(j + 1 < NC)
             def _():
                 stage3(j + 1)
-
-            send_first(j)
 
             @pl.when(j + 2 < NC)
             def _():
@@ -397,14 +405,16 @@
         def _():
             stage4(j + 1)
 
-    for s in range(PAGES):
-        slot, pair = tab[T_F + s], tab[T_J + s]
+    for p in range(PAGES):
+        slot, chip = tab[T_F + p], tab[T_J + p]
         for n in range(NC):
-            out[s, :, n * CW:(n + 1) * CW] = fin[((n + NC - pair) % NC) * NS + slot]
+            o = (n + NZ - chip) % NZ
+            s = jnp.where(o == 0, 0, jnp.where(o <= NZ // 2, 2 * o - 1, 2 * (NZ - o)))
+            out[p, :, n * CW:(n + 1) * CW] = fin[s * NS + slot]
 
     pair_copy.wait_send()
-    for k in range(NZ - 1):
-        z_copy(k).wait_send()
+    for k in range(1, NC):
+        arrived(one, z_s.at[k])
 
     @pl.loop(0, NC)
     def _(s):
@@ -434,7 +444,6 @@
 def local(hidden, lengths, kv_weight, input_gain, key_gain):
     rows, depth = hidden.shape
     piece = depth // 16
-    g, t = lax.axis_index("grp"), lax.axis_index("tp")
     vm, sm, anym = (pl.BlockSpec(memory_space=s) for s in (pltpu.VMEM, pltpu.SMEM, pl.ANY))
     tab = pl.pallas_call(
         table_kernel,
@@ -444,23 +453,21 @@
         scratch_shapes=[pltpu.SMEM((2 * NZ + 1,), I32)],
         name="tables",
     )(lengths)
-    gain = lax.dynamic_slice(input_gain, (g * piece,), (piece,))
-    scaled = (kv_weight.astype(F32) * gain[:, None]).astype(BF)
-    lane = lax.broadcasted_iota(I32, (piece, HD), 1) // (HD // 2)
-    wp = jnp.where(lane == t % 2, jnp.concatenate([scaled, scaled], axis=1), jnp.zeros((), BF))
     blk = lambda *s: pltpu.VMEM((*s, BLK, CW), BF)
     dma = lambda *s: pltpu.SemaphoreType.DMA(s)
     half = piece // 2
-    return pl.pallas_call(
+    pages = pl.pallas_call(
         functools.partial(main_kernel, rows, depth),
         out_shape=jax.ShapeDtypeStruct((PAGES, BLK, NC * CW), BF),
-        in_specs=[sm, vm, vm, anym, anym],
+        in_specs=[sm, vm, vm, vm, anym, anym],
         out_specs=vm,
         scratch_shapes=[
             pltpu.VMEM((rows, depth), BF),
             pltpu.VMEM((2, rows, HD), F32),
             pltpu.VMEM((rows, HD), F32),
             pltpu.VMEM((NZ, 4, 4, 2, half, HD), BF),
+            pltpu.VMEM((HD, piece + HD // 2), F32),
+            pltpu.VMEM((piece, HD), BF),
             pltpu.VMEM((half, HD), BF),
             blk(NB),
             pltpu.VMEM((3 * BLK, CW), F32),
@@ -473,8 +480,8 @@
             *[blk(NC, s) for s in CB],
             dma(NB),
             *[pltpu.SemaphoreType.DMA] * 3,
-            dma(NZ - 1),
-            dma(NZ),
+            dma(NC),
+            dma(NC),
             *[dma(NC, 2)] * 4,
             *[dma(NC, 2, 4)] * 3,
             dma(NC, 2),
@@ -487,7 +494,9 @@
             collective_id=0, has_side_effects=True, vmem_limit_bytes=66_000_000
         ),
         name="recompute",
-    )(tab, wp, key_gain[None, :], jnp.asarray(rotary(rows)), hidden)
+    )(tab, kv_weight.T, input_gain[None, :], key_gain[None, :], jnp.asarray(rotary(rows)), hidden)
+    live = tab[T_F:T_F + PAGES] != ZERO
+    return jnp.where(live[:, None, None], pages, jnp.zeros((), BF))
 
 
 def solution(mesh):

time: 128 us -> 153 us (1.20); the launches traced: 128 us -> 150 us
  Pallas kernels: 123 us -> 147 us
  local copies, waits for them, and re-layouts: 4.19 us -> 0 us
  other arithmetic: 0.85 us -> 3.26 us
    pallas_call x1, Pallas kernels: 121 us -> 146 us  [local(): pl.pallas_call(functools.partial(main_kernel, rows, depth), out_shape=jax...]
    unnamed x1 -> x0, local copies, waits for them, and re-layouts: 2.52 us -> none
    select_n x1, other arithmetic: 0.73 us -> 2.53 us  [local(): return jnp.where(live[:, None, None], pages, jnp.zeros((), BF))]
where the time goes in v3:
time: 153 us; the launch traced here: 150 us
  Pallas kernels  147 us (96%)
  other arithmetic  3.26 us (2%)
    pallas_call x1, Pallas kernels, local(): pl.pallas_call(functools.partial(main_kernel, rows, depth), out_shape=jax...  146 us

profile of v3, /device:TPU:1, one launch (start us, length us, event | category | flops | bytes accessed | tf_op | source)
XLA Modules:
  0.0 150.5 jit_solution(6786410141101189820)
XLA Ops:
  0.0 1.6 %tables.1.refs_0_ = s32[32]{0:T(128)} custom-call(s32[1,16]{1,0:T(1,128)} %len_ref.1), custom_call_target="tpu_custom_call" | custom-call | tf_op jit(solution)/shard_map/tables/pallas_call | solution.py:448
  1.6 0.7 slice_compare_fusion
  2.4 145.6 %recompute.1 = bf16[5,128,1024]{2,1,0:T(8,128)(2,1)} custom-call(s32[32]{0:T(128)} %tables.1.refs_0_, bf16[64,320]{1,0:T(8,128)(2,1)} %bitcast.3, f32[1,5120]{1,0:T(1,128)} %bitcast.4, f32[1,128]{1,0:T(1,128)} %bitcast.5, f32[2,1152,128]{2,1,0:T(8,128)} %constant.6.clone.refs_4_, bf16[1152,5120]{1,0:T(8,128)(2,1)} %refs_5_.1), custom_call_target="tpu_custom_call" | custom-call | tf_op jit(solution)/shard_map/recompute/pallas_call | solution.py:459
  147.9 2.5 %broadcast_select_fusion = bf16[5,128,1024]{2,1,0:T(8,128)(2,1)} fusion(bf16[5,128,1024]{2,1,0:T(8,128)(2,1)} %recompute.1, pred[5]{0:T(512)(128)(4,1)S(1)} %slice_compare_fusion), kind=kLoop, calls=%fused_computation | loop fusion | flops 655360 | bytes 2621445 | tf_op jit(solution)/shard_map/jit(_where)/select_n | solution.py:499

commit v4 on v3

--- a/solution.py
+++ b/solution.py
@@ -135,18 +135,14 @@
     far = dev(g, 2 * ((z + d + NZ) % NZ) + c)
     near = dev(g, 2 * ((z - d + NZ) % NZ) + c)
 
-    def at(a, b):
-        yy = (y + jnp.where(c == 0, b, a) + 4) % 4
-        xx = (x + jnp.where(c == 0, a, b) + 4) % 4
-        return yy, xx
-
-    def peer(a, b):
-        yy, xx = at(a, b)
-        return dev(yy * 4 + xx, t)
+    p, q = jnp.where(c == 0, x, y), jnp.where(c == 0, y, x)
+
+    def peer(i, j):
+        i, j = (p + i + 4) % 4, (q + j + 4) % 4
+        return dev(jnp.where(c == 0, j * 4 + i, i * 4 + j), t)
 
     first = (peer(1, 0), peer(-1, 0))
     second = (peer(0, 1), peer(0, -1))
-    offsets = (0, -1, 1, 2)
 
     def x_copy(b):
         rows_b = pl.ds(pl.multiple_of(b * BLK, BLK), BLK)
@@ -162,8 +158,8 @@
 
     barrier = pltpu.get_barrier_semaphore()
     everyone = [partner, above, below, *first, *second]
-    for p in everyone:
-        pl.semaphore_signal(barrier, inc=1, device_id=p, device_id_type=MESH)
+    for other in everyone:
+        pl.semaphore_signal(barrier, inc=1, device_id=other, device_id_type=MESH)
 
     piece_k = depth // 16
     odd = (g * piece_k) % HD
@@ -190,59 +186,50 @@
     pair_copy.start()
     pair_copy.wait_recv()
     mine = wp[pl.ds(pl.multiple_of(c * half, half), half)]
-    W[z, y, x, c] = mine + pairb[...]
+    W[z, c, q, p] = mine + pairb[...]
 
     def unit(s):
         return (z + jnp.where(s % 2 == 1, (s + 1) // 2, NZ - s // 2)) % NZ
 
-    def piece(s, a, b):
-        yy, xx = at(a, b)
-        return W.at[unit(s), yy, xx, c]
-
-    def part(s, a, b, h):
-        yy, xx = at(a, b)
-        return W.at[unit(s), yy, xx, c, pl.ds(h * quarter, quarter)]
+    def piece(s, i):
+        return W.at[unit(s), c, q, (p + i + 4) % 4]
+
+    def row(s, j):
+        return W.at[unit(s), c, (q + j + 4) % 4]
 
     def p1_copy(s, v):
-        return remote(piece(s, 0, 0), piece(s, 0, 0), p1_s.at[s, v], p1_r.at[s, v], first[v])
+        return remote(piece(s, 0), piece(s, 0), p1_s.at[s, v], p1_r.at[s, v], first[v])
 
     def p1h_copy(s, v):
-        w = part(s, -1 if v == 0 else 1, 0, v)
+        w = piece(s, 2 * v - 1).at[pl.ds(v * quarter, quarter)]
         return remote(w, w, p1h_s.at[s, v], p1h_r.at[s, v], first[v])
 
-    def p2_copy(s, v, i):
-        w = piece(s, offsets[i], 0)
-        return remote(w, w, p2_s.at[s, v, i], p2_r.at[s, v, i], second[v])
-
-    def p2h_copy(s, v, i):
-        w = part(s, offsets[i], -1 if v == 0 else 1, v)
-        return remote(w, w, p2h_s.at[s, v, i], p2h_r.at[s, v], second[v])
-
-    def hand_copy(s, i, j):
-        w = piece(s, offsets[i], offsets[j])
-        return remote(w, w, h_s.at[s, i, j], h_r.at[s], partner)
+    def p2_copy(s, v):
+        return remote(row(s, 0), row(s, 0), p2_s.at[s, v], p2_r.at[s, v], second[v])
+
+    def p2h_copy(s, v):
+        w = row(s, 2 * v - 1).at[pl.ds(2 * v, 2)]
+        return remote(w, w, p2h_s.at[s, v], p2h_r.at[s, v], second[v])
+
+    def hand_copy(s, j):
+        return remote(row(s, j), row(s, j), h_s.at[s, j + 1], h_r.at[s], partner)
 
     one = W.at[0, 0, 0, 0]
-    one_part = W.at[0, 0, 0, 0, pl.ds(0, quarter)]
-    four_parts = W.at[0, 0, :, 0, pl.ds(0, quarter)]
-    whole_half = W.at[0, :, :, 0]
-
-    def send_row(s, i):
-        for v in range(2):
-            p2_copy(s, v, i).start()
-        hand_copy(s, i, 0).start()
+    one_part = one.at[pl.ds(0, quarter)]
+    one_row = W.at[0, 0, 0]
+    two = W.at[0, 0, 0, pl.ds(0, 2)]
+    whole_half = W.at[0, 0]
 
     def z_pass(s, to, up):
-        w = W.at[unit(s), y, x, c]
-        return remote(w, w, z_s.at[to], z_r.at[to], above if up else below)
+        return remote(piece(s, 0), piece(s, 0), z_s.at[to], z_r.at[to], above if up else below)
 
     def stage1(s):
         for v in range(2):
             p1_copy(s, v).start()
-        send_row(s, 0)
 
     def z_step(s):
         arrived(one, z_r.at[s])
+        stage1(s)
 
         @pl.when((s % 2 == 1) & (s + 2 < NC))
         def _():
@@ -252,29 +239,28 @@
         def _():
             z_pass(s, s + 2, True).start()
 
-        stage1(s)
-
     def stage2(s):
         for v in range(2):
             arrived(one, p1_r.at[s, v])
             p1h_copy(s, v).start()
-            send_row(s, 1 + v)
 
     def stage3(s):
         for v in range(2):
             arrived(one_part, p1h_r.at[s, v])
-        send_row(s, 3)
-        for i in range(4):
-            for v in range(2):
-                arrived(one, p2_r.at[s, v, i])
-                p2h_copy(s, v, i).start()
-                hand_copy(s, i, 1 + v).start()
+        for v in range(2):
+            p2_copy(s, v).start()
+        hand_copy(s, 0).start()
 
     def stage4(s):
         for v in range(2):
-            arrived(four_parts, p2h_r.at[s, v])
-        for i in range(4):
-            hand_copy(s, i, 3).start()
+            arrived(one_row, p2_r.at[s, v])
+            p2h_copy(s, v).start()
+            hand_copy(s, 2 * v - 1).start()
+
+    def stage5(s):
+        for v in range(2):
+            arrived(two, p2h_r.at[s, v])
+        hand_copy(s, 2).start()
 
     length = tab[T_LEN]
 
@@ -293,18 +279,23 @@
             p = r0 + lax.broadcasted_iota(I32, (BLK, HD), 0)
             rs[rows_b, :] = jnp.where(p < length, scale, 0.0)
 
+    stage1(0)
     z_pass(0, 1, False).start()
     z_pass(0, 2, True).start()
-    stage1(0)
     row_scales(0, 2)
     stage2(0)
+    z_step(1)
     row_scales(2, 4)
     stage3(0)
-    z_step(1)
+    stage2(1)
     row_scales(4, 6)
     stage4(0)
-    stage2(1)
+    stage3(1)
+    z_step(2)
     row_scales(6, NB)
+    stage5(0)
+    stage4(1)
+    stage2(2)
     cs_copy.wait()
     for j in range(NC):
         fin[j * NS + ZERO] = jnp.zeros((BLK, CW), BF)
@@ -317,7 +308,9 @@
         def _(i):
             r0 = pl.multiple_of(i * tile, tile)
             rows_i = pl.ds(r0, tile)
-            a = jnp.dot(xv[rows_i, :], W[n].reshape(depth, HD), preferred_element_type=F32)
+            w = [W[n, 0, gg // 4, gg % 4] if cc == 0 else W[n, 1, gg % 4, gg // 4]
+                 for gg in range(16) for cc in range(2)]
+            a = jnp.dot(xv[rows_i, :], jnp.concatenate(w, axis=0), preferred_element_type=F32)
             acc[...] = a * rs[rows_i, :]
 
             @pl.when(n < NC // 2)
@@ -343,21 +336,23 @@
         s = stb.at[j] if h == 0 else rb[h - 1].at[j, pl.ds(0, CB[h])]
         return remote(s, rb[h].at[j], a2a_s.at[j, 5 + h], a2a_r.at[j, 5 + h], near)
 
-    def send_first(j):
-        base = j * NS
+    def send_pair(j):
         for e in range(5):
             stp[j, e] = own[tab[T_P + e]]
         pair_block_copy(j).start()
         for e in range(5):
-            fin[base + e] = own[tab[T_O + e]]
+            fin[j * NS + e] = own[tab[T_O + e]]
+
+    def send_first(j):
+        base = j * NS
         pair_block_copy(j).wait_recv()
         for e in range(5):
             fin[base + 5 + e] = prv[j, e]
-        for q in range(CA[0]):
-            sta[j, q] = fin[base + tab[T_A + q]]
+        for e in range(CA[0]):
+            sta[j, e] = fin[base + tab[T_A + e]]
         hop_a(j, 0).start()
-        for q in range(CB[0]):
-            stb[j, q] = fin[base + tab[T_B + q]]
+        for e in range(CB[0]):
+            stb[j, e] = fin[base + tab[T_B + e]]
         hop_b(j, 0).start()
 
     def forward(j, h):
@@ -375,42 +370,36 @@
             for q in range(CB[h - 1]):
                 fin[base + BASE_B[h - 1] + q] = rb[h - 1][j, q]
 
+    def step_in_range(stage, s):
+        @pl.when(s < NC)
+        def _():
+            stage(s)
+
     @pl.loop(0, NC + 4)
     def _(j):
         @pl.when(j < NC)
         def _():
             arrived(whole_half, h_r.at[j])
-
-            @pl.when(j + 2 < NC)
-            def _():
-                z_step(j + 2)
-
+            step_in_range(stage5, j + 1)
+            step_in_range(stage3, j + 2)
+            step_in_range(z_step, j + 3)
             compute(j)
+            send_pair(j)
+            step_in_range(stage4, j + 2)
+            step_in_range(stage2, j + 3)
             send_first(j)
-
-            @pl.when(j + 1 < NC)
-            def _():
-                stage3(j + 1)
-
-            @pl.when(j + 2 < NC)
-            def _():
-                stage2(j + 2)
 
         for h in (1, 2, 3, 4):
             @pl.when((j - h >= 0) & (j - h < NC))
             def _():
                 forward(j - h, h)
 
-        @pl.when(j + 1 < NC)
-        def _():
-            stage4(j + 1)
-
-    for p in range(PAGES):
-        slot, chip = tab[T_F + p], tab[T_J + p]
+    for page in range(PAGES):
+        slot, chip = tab[T_F + page], tab[T_J + page]
         for n in range(NC):
             o = (n + NZ - chip) % NZ
             s = jnp.where(o == 0, 0, jnp.where(o <= NZ // 2, 2 * o - 1, 2 * (NZ - o)))
-            out[p, :, n * CW:(n + 1) * CW] = fin[s * NS + slot]
+            out[page, :, n * CW:(n + 1) * CW] = fin[s * NS + slot]
 
     pair_copy.wait_send()
     for k in range(1, NC):
@@ -421,12 +410,10 @@
         for v in range(2):
             p1_copy(s, v).wait_send()
             p1h_copy(s, v).wait_send()
-            for i in range(4):
-                p2_copy(s, v, i).wait_send()
-                p2h_copy(s, v, i).wait_send()
-        for i in range(4):
-            for j in range(4):
-                hand_copy(s, i, j).wait_send()
+            p2_copy(s, v).wait_send()
+            p2h_copy(s, v).wait_send()
+        for j in (-1, 0, 1, 2):
+            hand_copy(s, j).wait_send()
         pair_block_copy(s).wait_send()
         for h in range(4):
             hop_a(s, h).wait_send()
@@ -465,7 +452,7 @@
             pltpu.VMEM((rows, depth), BF),
             pltpu.VMEM((2, rows, HD), F32),
             pltpu.VMEM((rows, HD), F32),
-            pltpu.VMEM((NZ, 4, 4, 2, half, HD), BF),
+            pltpu.VMEM((NZ, 2, 4, 4, half, HD), BF),
             pltpu.VMEM((HD, piece + HD // 2), F32),
             pltpu.VMEM((piece, HD), BF),
             pltpu.VMEM((half, HD), BF),
@@ -482,10 +469,8 @@
             *[pltpu.SemaphoreType.DMA] * 3,
             dma(NC),
             dma(NC),
-            *[dma(NC, 2)] * 4,
-            *[dma(NC, 2, 4)] * 3,
-            dma(NC, 2),
-            dma(NC, 4, 4),
+            *[dma(NC, 2)] * 8,
+            dma(NC, 4),
             dma(NC),
             dma(NC, 8),
             dma(NC, 8),

time: 153 us -> 128 us (0.84)
  Pallas kernels: 147 us -> 124 us
    pallas_call x1, Pallas kernels: 146 us -> 122 us  [local(): pl.pallas_call(functools.partial(main_kernel, rows, depth), out_shape=jax...]
where the time goes in v4:
time: 128 us; the launch traced here: 127 us
  Pallas kernels  124 us (97%)
  other arithmetic  3.26 us (3%)
    pallas_call x1, Pallas kernels, local(): pl.pallas_call(functools.partial(main_kernel, rows, depth), out_shape=jax...  122 us

profile of v4, /device:TPU:1, one launch (start us, length us, event | category | flops | bytes accessed | tf_op | source)
XLA Modules:
  0.0 127.0 jit_solution(11977064643140036869)
XLA Ops:
  0.0 1.6 %tables.1.refs_0_ = s32[32]{0:T(128)} custom-call(s32[1,16]{1,0:T(1,128)} %len_ref.1), custom_call_target="tpu_custom_call" | custom-call | tf_op jit(solution)/shard_map/tables/pallas_call | solution.py:435
  1.6 0.7 slice_compare_fusion
  2.4 122.0 %recompute.1 = bf16[5,128,1024]{2,1,0:T(8,128)(2,1)} custom-call(s32[32]{0:T(128)} %tables.1.refs_0_, bf16[64,320]{1,0:T(8,128)(2,1)} %bitcast.3, f32[1,5120]{1,0:T(1,128)} %bitcast.4, f32[1,128]{1,0:T(1,128)} %bitcast.5, f32[2,1152,128]{2,1,0:T(8,128)} %constant.6.clone.refs_4_, bf16[1152,5120]{1,0:T(8,128)(2,1)} %refs_5_.1), custom_call_target="tpu_custom_call" | custom-call | tf_op jit(solution)/shard_map/recompute/pallas_call | solution.py:446
  124.4 2.5 %broadcast_select_fusion = bf16[5,128,1024]{2,1,0:T(8,128)(2,1)} fusion(bf16[5,128,1024]{2,1,0:T(8,128)(2,1)} %recompute.1, pred[5]{0:T(512)(128)(4,1)S(1)} %slice_compare_fusion), kind=kLoop, calls=%fused_computation | loop fusion | flops 655360 | bytes 2621445 | tf_op jit(solution)/shard_map/jit(_where)/select_n | solution.py:484

commit v5 on v4

--- a/solution.py
+++ b/solution.py
@@ -288,14 +288,14 @@
     row_scales(2, 4)
     stage3(0)
     stage2(1)
+    z_step(2)
     row_scales(4, 6)
     stage4(0)
     stage3(1)
-    z_step(2)
+    stage2(2)
     row_scales(6, NB)
     stage5(0)
-    stage4(1)
-    stage2(2)
+    z_step(3)
     cs_copy.wait()
     for j in range(NC):
         fin[j * NS + ZERO] = jnp.zeros((BLK, CW), BF)
@@ -380,19 +380,41 @@
         @pl.when(j < NC)
         def _():
             arrived(whole_half, h_r.at[j])
-            step_in_range(stage5, j + 1)
-            step_in_range(stage3, j + 2)
-            step_in_range(z_step, j + 3)
             compute(j)
             send_pair(j)
-            step_in_range(stage4, j + 2)
+
+            @pl.when(j == 0)
+            def _():
+                stage4(1)
+                stage3(2)
+
+            @pl.when((j > 0) & (j + 2 < NC))
+            def _():
+                stage4(j + 2)
+
             step_in_range(stage2, j + 3)
             send_first(j)
+            step_in_range(z_step, j + 4)
+
+            @pl.when(j == 0)
+            def _():
+                stage5(1)
+                stage4(2)
+
+            @pl.when(j == 1)
+            def _():
+                stage5(2)
 
         for h in (1, 2, 3, 4):
             @pl.when((j - h >= 0) & (j - h < NC))
             def _():
                 forward(j - h, h)
+
+        step_in_range(stage3, j + 3)
+
+        @pl.when((j > 0) & (j + 2 < NC))
+        def _():
+            stage5(j + 2)
 
     for page in range(PAGES):
         slot, chip = tab[T_F + page], tab[T_J + page]

time: 128 us -> 122 us (0.953)
  Pallas kernels: 124 us -> 118 us
    pallas_call x1, Pallas kernels: 122 us -> 117 us  [local(): pl.pallas_call(functools.partial(main_kernel, rows, depth), out_shape=jax...]
where the time goes in v5:
time: 122 us
  Pallas kernels  118 us (97%)
  other arithmetic  3.26 us (3%)
    pallas_call x1, Pallas kernels, local(): pl.pallas_call(functools.partial(main_kernel, rows, depth), out_shape=jax...  117 us
    select_n x1, other arithmetic, local(): return jnp.where(live[:, None, None], pages, jnp.zeros((), BF))  2.53 us

profile of v5, /device:TPU:1, one launch (start us, length us, event | category | flops | bytes accessed | tf_op | source)
XLA Modules:
  0.0 121.6 jit_solution(16061826565404348186)
XLA Ops:
  0.0 1.6 %tables.1.refs_0_ = s32[32]{0:T(128)} custom-call(s32[1,16]{1,0:T(1,128)} %len_ref.1), custom_call_target="tpu_custom_call" | custom-call | tf_op jit(solution)/shard_map/tables/pallas_call | solution.py:457
  1.6 0.7 slice_compare_fusion
  2.4 116.7 %recompute.1 = bf16[5,128,1024]{2,1,0:T(8,128)(2,1)} custom-call(s32[32]{0:T(128)} %tables.1.refs_0_, bf16[64,320]{1,0:T(8,128)(2,1)} %bitcast.3, f32[1,5120]{1,0:T(1,128)} %bitcast.4, f32[1,128]{1,0:T(1,128)} %bitcast.5, f32[2,1152,128]{2,1,0:T(8,128)} %constant.6.clone.refs_4_, bf16[1152,5120]{1,0:T(8,128)(2,1)} %refs_5_.1), custom_call_target="tpu_custom_call" | custom-call | tf_op jit(solution)/shard_map/recompute/pallas_call | solution.py:468
  119.1 2.5 %broadcast_select_fusion = bf16[5,128,1024]{2,1,0:T(8,128)(2,1)} fusion(bf16[5,128,1024]{2,1,0:T(8,128)(2,1)} %recompute.1, pred[5]{0:T(512)(128)(4,1)S(1)} %slice_compare_fusion), kind=kLoop, calls=%fused_computation | loop fusion | flops 655360 | bytes 2621445 | tf_op jit(solution)/shard_map/jit(_where)/select_n | solution.py:506
